TPU v7x, 32 devices: a whole 2x2x4 slice. The times are simulated.
32 devices in a mesh: gx: 4 (over x, core), gy: 2 (over y), orb: 4 (over z).
Axes of the slice: x: 2, y: 2, z: 4, core: 2. Of those that a mesh axis runs over, the one named last changes fastest.
Arguments:
- orbitals: float32 [4, 32, 32, 384], P('orb', 'gx', 'gy'), may hold values from -6 to 6
- local_pot: float32 [32, 32, 384], P('gx', 'gy'), may hold values from -1 to 1
- proj_vals: bfloat16 [4, 32, 32, 384], P(None, 'gx', 'gy'), may hold values from -0.29882812 to 0.29882812
- proj_ids: int32 [4, 32, 32, 3], P(None, 'gx', 'gy'), may hold values from 0 to 4095, as said below
- proj_energy: float32 [4096], replicated, may hold values from 0.5 to 2
- cheb_coef: float32 [4], replicated, may hold values from 0.2 to 1
Outputs:
- density: float32 [32, 32, 384], P('gx', 'gy')
Inputs may be any that keep to these rules, and one draw needn't show every extreme that they name: `proj_ids`: the owner o = id // 512 of each id names the column block (o // 2, o % 2); it differs from the block (x // 8, y // 16) of the slot's cells by at most one in each of the two coordinates, periodically.
All inputs are finite; a program needn't handle non-finite values.
Results may differ from a plain program's by a relative error of at most 0.0003.
Values sent between devices are 32-bit elements; how exact they have to be, the bound alone decides.
No kernel may reach another device: no remote copies, remote signals or barrier semaphores. Data moves between devices by JAX's collectives and lax.ppermute only.
A program may use at most 64 MiB of HBM per device.

v0:
```python
import jax
import jax.numpy as jnp
from jax import lax
from jax.sharding import PartitionSpec as P

ZB = 128
STEPS = 3
E_MID = 4.0
E_HALF = 8.0
PRECISE = lax.Precision.HIGHEST


def extended(block, sides, width):
    for axis, dim in sides:
        count = lax.axis_size(axis)
        forward = [(i, i + 1) for i in range(count - 1)]
        forward.append((count - 1, 0))
        backward = [(target, source) for source, target in forward]
        low = lax.ppermute(
            lax.slice_in_dim(block, block.shape[dim] - width, None, axis=dim), axis, forward
        )
        high = lax.ppermute(lax.slice_in_dim(block, 0, width, axis=dim), axis, backward)
        block = jnp.concatenate([low, block, high], axis=dim)
    return block


def stencil(grid_vals):
    extent_first = grid_vals.shape[1]
    extent_second = grid_vals.shape[2]
    padded = extended(grid_vals, (("gx", 1), ("gy", 2)), 2)
    middle_rows = padded[:, :, 2 : 2 + extent_second]
    middle_cols = padded[:, 2 : 2 + extent_first]
    result = -90.0 * grid_vals
    result = (
        result
        + 16.0 * (middle_rows[:, 1 : 1 + extent_first] + middle_rows[:, 3 : 3 + extent_first])
        - (middle_rows[:, 0:extent_first] + middle_rows[:, 4 : 4 + extent_first])
    )
    result = (
        result
        + 16.0
        * (middle_cols[:, :, 1 : 1 + extent_second] + middle_cols[:, :, 3 : 3 + extent_second])
        - (middle_cols[:, :, 0:extent_second] + middle_cols[:, :, 4 : 4 + extent_second])
    )
    result = (
        result
        + 16.0 * (jnp.roll(grid_vals, 1, 3) + jnp.roll(grid_vals, -1, 3))
        - (jnp.roll(grid_vals, 2, 3) + jnp.roll(grid_vals, -2, 3))
    )
    return result / 12.0


def local(orbitals, local_pot, proj_vals, proj_ids, proj_energy, cheb_coef):
    count_orb = orbitals.shape[0]
    extent_first = orbitals.shape[1]
    extent_second = orbitals.shape[2]
    extent_depth = orbitals.shape[3]
    slot_count = proj_vals.shape[0]
    block_count = extent_depth // ZB
    count_all = proj_energy.shape[0]
    shaped = proj_vals.astype(jnp.float32).reshape(
        slot_count, extent_first, extent_second, block_count, ZB
    )
    ids_flat = proj_ids.reshape(-1)

    def weights_of(blocks):
        partial_value = jax.vmap(
            lambda single: jax.ops.segment_sum(single, ids_flat, num_segments=count_all)
        )(blocks.reshape(count_orb, -1))
        coef_sums = lax.psum(partial_value, ("gx", "gy"))
        return jnp.take(coef_sums * proj_energy[None, :], ids_flat, axis=1)

    def hamilton(grid_vals):
        blocks = jnp.einsum(
            "kxyzb,oxyzb->okxyz",
            shaped,
            grid_vals.reshape(count_orb, extent_first, extent_second, block_count, ZB),
            precision=PRECISE,
        )
        weights = weights_of(blocks).reshape(
            count_orb, slot_count, extent_first, extent_second, block_count
        )
        projected = jnp.einsum("kxyzb,okxyz->oxyzb", shaped, weights, precision=PRECISE).reshape(
            grid_vals.shape
        )
        return (
            -0.5 * stencil(grid_vals) + local_pot[None] * grid_vals + projected - E_MID * grid_vals
        ) / E_HALF

    previous = orbitals
    current = hamilton(orbitals)
    filtered = cheb_coef[0] * previous + cheb_coef[1] * current
    for degree in range(2, STEPS + 1):
        following = 2.0 * hamilton(current) - previous
        previous = current
        current = following
        filtered = filtered + cheb_coef[degree] * current
    density = lax.psum(jnp.sum(filtered * filtered, axis=0), "orb")
    return density / (count_orb * lax.axis_size("orb"))


def solution(mesh):
    return jax.shard_map(
        local,
        mesh=mesh,
        in_specs=(
            P("orb", "gx", "gy", None),
            P("gx", "gy", None),
            P(None, "gx", "gy", None),
            P(None, "gx", "gy", None),
            P(),
            P(),
        ),
        out_specs=P("gx", "gy", None),
        check_vma=False,
    )
```

profile of v0, /device:TPU:0, one launch (start us, length us, event | category | flops | bytes accessed | tf_op | source)
XLA Modules:
  0.0 220.9 jit_solution(10837765373750434986)
XLA Ops:
  6.5 0.9 fusion.72
  7.4 0.5 collective-permute-start
  7.9 2.0 collective-permute-start.1
  9.9 0.2 reshape.498
  10.1 0.1 fusion.74
  10.4 0.8 copy-done.2
  11.3 0.5 copy.9
  11.9 1.4 fusion.78
  13.2 1.0 copy.10
  14.3 0.2 reshape.440
  14.5 0.6 copy-done.4
  15.1 0.3 copy.7
  15.3 0.2 reshape.438
  15.6 8.6 %scatter_custom_fusion = f32[4096]{0:T(1024)S(1)} fusion(s32[1536]{0:T(1024)S(1)} %reshape.438, f32[1536]{0:T(1024)S(1)} %reshape.440, f32[]{:T(128)} %constant.38.clone.1), kind=kCustom, calls=%fused_computation.125 | custom fusion | flops 1536 | bytes 16388 | tf_op jit(solution)/shard_map/vmap()/scatter-add | solution.py:68
  24.2 24.7 %psum.28 = f32[1,4096]{1,0:T(1,128)S(1)} all-reduce(f32[1,4096]{1,0:T(1,128)S(1)} %bitcast.82), channel_id=1, replica_groups=mesh['gx'=4,'gy'=2,'orb'=4] {'gx','gy'}, use_global_device_ids=true, to_apply=%region_1.0 | all-reduce | flops 4096 | bytes 32768 | tf_op jit(solution)/shard_map/psum | solution.py:70
  48.9 0.7 copy-done.3
  49.6 8.4 %gather_fusion = f32[1536]{0:T(1024)S(1)} fusion(f32[4096]{0:T(1024)S(1)} %bitcast.70, s32[2048]{0:T(1024)S(1)} %pad_clamp_fusion), kind=kCustom, calls=%fused_computation.clone | custom fusion | bytes 18432 | tf_op jit(solution)/shard_map/jit(_take)/gather | solution.py:71
  58.0 0.2 reshape.487
  58.2 0.9 copy.11
  59.1 1.4 fusion.79
  60.7 0.1 collective-permute-start.2
  60.9 2.0 collective-permute-start.3
  62.8 0.6 fusion.77
  64.3 0.5 collective-permute-done.2
  64.8 0.4 collective-permute-done.3
  65.2 0.6 copy-done.5
  65.8 1.1 broadcast_multiply_fusion.1
  66.9 0.2 reshape.502
  67.2 0.1 fusion.69
  67.4 1.7 collective-permute-start.5
  69.2 1.4 fusion.80
  70.5 1.0 copy.14
  71.6 0.2 reshape.450
  71.8 8.6 %scatter_custom_fusion.1 = f32[4096]{0:T(1024)S(1)} fusion(s32[1536]{0:T(1024)S(1)} %reshape.438, f32[1536]{0:T(1024)S(1)} %reshape.450, f32[]{:T(128)} %constant.38.clone.1), kind=kCustom, calls=%fused_computation.123 | custom fusion | flops 1536 | bytes 16388 | tf_op jit(solution)/shard_map/vmap()/scatter-add | solution.py:68
  80.4 24.0 %psum.29 = f32[1,4096]{1,0:T(1,128)S(1)} all-reduce(f32[1,4096]{1,0:T(1,128)S(1)} %bitcast.83), channel_id=1, replica_groups=mesh['gx'=4,'gy'=2,'orb'=4] {'gx','gy'}, use_global_device_ids=true, to_apply=%region_3.5 | all-reduce | flops 4096 | bytes 32768 | tf_op jit(solution)/shard_map/psum | solution.py:70
  104.4 8.4 %gather_fusion.1 = f32[1536]{0:T(1024)S(1)} fusion(f32[4096]{0:T(1024)S(1)} %bitcast.71, s32[2048]{0:T(1024)S(1)} %pad_clamp_fusion), kind=kCustom, calls=%fused_computation.1.clone | custom fusion | bytes 18432 | tf_op jit(solution)/shard_map/jit(_take)/gather | solution.py:71
  112.8 0.2 reshape.491
  113.0 0.9 copy.15
  113.9 1.4 fusion.81
  115.5 0.7 collective-permute-start.6
  116.1 1.4 collective-permute-start.7
  117.8 1.7 collective-permute-done.6
  119.5 0.6 collective-permute-done.7
  120.1 0.3 fusion.30
  120.4 0.2 reshape.506
  120.6 0.1 fusion.64
  120.7 0.1 fusion.66
  120.9 1.7 collective-permute-start.9
  122.7 1.4 fusion.82
  124.0 1.0 copy.18
  125.1 0.2 reshape.460
  125.3 8.6 %scatter_custom_fusion.2 = f32[4096]{0:T(1024)S(1)} fusion(s32[1536]{0:T(1024)S(1)} %reshape.438, f32[1536]{0:T(1024)S(1)} %reshape.460, f32[]{:T(128)} %constant.38.clone.1), kind=kCustom, calls=%fused_computation.121 | custom fusion | flops 1536 | bytes 16388 | tf_op jit(solution)/shard_map/vmap()/scatter-add | solution.py:68
  133.9 23.8 %psum.30 = f32[1,4096]{1,0:T(1,128)S(1)} all-reduce(f32[1,4096]{1,0:T(1,128)S(1)} %bitcast.81), channel_id=1, replica_groups=mesh['gx'=4,'gy'=2,'orb'=4] {'gx','gy'}, use_global_device_ids=true, to_apply=%region_5.7 | all-reduce | flops 4096 | bytes 32768 | tf_op jit(solution)/shard_map/psum | solution.py:70
  157.7 8.4 %gather_fusion.2 = f32[1536]{0:T(1024)S(1)} fusion(f32[4096]{0:T(1024)S(1)} %bitcast.69, s32[2048]{0:T(1024)S(1)} %pad_clamp_fusion), kind=kCustom, calls=%fused_computation.2.clone | custom fusion | bytes 18432 | tf_op jit(solution)/shard_map/jit(_take)/gather | solution.py:71
  166.1 0.2 reshape.495
  166.3 0.9 copy.19
  167.2 1.4 fusion.83
  168.7 0.9 collective-permute-start.10
  169.6 1.2 collective-permute-start.11
  171.1 1.7 collective-permute-done.10
  172.8 0.8 collective-permute-done.11
  173.6 3.0 %multiply_bitcast_fusion = f32[8,16,384]{2,1,0:T(8,128)} fusion(f32[1,8,16,384]{3,2,1,0:T(8,128)S(1)} %fusion.30, f32[1,8,16,384]{3,2,1,0:T(8,128)S(1)} %get-tuple-element.7, f32[1,8,16,384]{3,2,1,0:T(8,128)S(1)} %copy-done, f32[1,8,16,384]{3,2,1,0:T(8,128)S(1)} %transpose.23, f32[8,16,384]{2,1,0:T(8,128)S(1)} %copy-done.1, ...), kind=kLoop, calls=%fused_computation.103 | loop fusion | flops 2605056 | bytes 2138128 | tf_op jit(solution)/shard_map/reduce_sum | solution.py:98
  176.6 35.8 %all-reduce.2.cloned.1.call-done = f32[8,16,384]{2,1,0:T(8,128)} async-done(((f32[8,16,384]{2,1,0:T(8,128)}), f32[8,16,384]{2,1,0:T(8,128)}) %all-reduce.2.cloned.1.call-update) | async-done | bytes 196624 | tf_op jit(solution)/shard_map/psum | solution.py:98
  212.4 1.6 broadcast_multiply_fusion
  (51 shorter events, 1.7 us)
Async XLA Ops:
  6.5 3.4 %copy-start = (f32[1,8,16,384]{3,2,1,0:T(8,128)S(1)}, f32[1,8,16,384]{3,2,1,0:T(8,128)}, u32[]{:S(2)}) copy-start(f32[1,8,16,384]{3,2,1,0:T(8,128)} %param.8) | copy-start | bytes 589828
  6.5 205.9 %all-reduce.2.cloned.1.call-start = ((), (), s32[]{:S(2)}) async-start(), calls=%async_computation | async-start | bytes 393216 | tf_op jit(solution)/shard_map/psum | solution.py:98
  7.4 53.2 %collective-permute-start = (f32[1,2,16,384]{3,2,1,0:T(8,128)S(1)}, f32[1,2,16,384]{3,2,1,0:T(8,128)S(1)}, u32[]{:S(2)}, u32[]{:S(2)}) collective-permute-start(f32[1,2,16,384]{3,2,1,0:T(8,128)S(1)} %get-tuple-element.40), channel_id=1, source_target_pairs={{0,8},{8,16},{16,24},{24,0},{1,9},{9,17},{17,25},{25,1},{2,10},{10... | collective-permute-start | bytes 147464 | tf_op jit(solution)/shard_map/ppermute | solution.py:19
  7.9 52.8 %collective-permute-start.1 = (f32[1,2,16,384]{3,2,1,0:T(8,128)S(1)}, f32[1,2,16,384]{3,2,1,0:T(8,128)S(1)}, u32[]{:S(2)}, u32[]{:S(2)}) collective-permute-start(f32[1,2,16,384]{3,2,1,0:T(8,128)S(1)} %get-tuple-element.39), channel_id=1, source_target_pairs={{8,0},{16,8},{24,16},{0,24},{9,1},{17,9},{25,17},{1,25},{10,2},{18... | collective-permute-start | bytes 147464 | tf_op jit(solution)/shard_map/ppermute | solution.py:22
  10.2 1.0 copy-start.2
  14.3 0.8 copy-start.4
  48.9 0.7 copy-start.3
  60.7 2.1 copy-start.6
  60.7 4.0 %collective-permute-start.2 = (f32[1,12,2,384]{3,2,1,0:T(2,128)S(1)}, f32[1,12,2,384]{3,2,1,0:T(2,128)S(1)}, u32[]{:S(2)}, u32[]{:S(2)}) collective-permute-start(f32[1,12,2,384]{3,2,1,0:T(2,128)S(1)} %get-tuple-element.14), channel_id=1, source_target_pairs={{0,4},{4,0},{1,5},{5,1},{2,6},{6,2},{3,7},{7,3},{8,12},{12,8},{9,1... | collective-permute-start | bytes 110600 | tf_op jit(solution)/shard_map/ppermute | solution.py:19
  60.9 4.3 %collective-permute-start.3 = (f32[1,12,2,384]{3,2,1,0:T(2,128)S(1)}, f32[1,12,2,384]{3,2,1,0:T(2,128)S(1)}, u32[]{:S(2)}, u32[]{:S(2)}) collective-permute-start(f32[1,12,2,384]{3,2,1,0:T(2,128)S(1)} %get-tuple-element.15), channel_id=1, source_target_pairs={{4,0},{0,4},{5,1},{1,5},{6,2},{2,6},{7,3},{3,7},{12,8},{8,12},{13,... | collective-permute-start | bytes 110600 | tf_op jit(solution)/shard_map/ppermute | solution.py:22
  63.5 2.2 %copy-start.1 = (f32[8,16,384]{2,1,0:T(8,128)S(1)}, f32[8,16,384]{2,1,0:T(8,128)}, u32[]{:S(2)}) copy-start(f32[8,16,384]{2,1,0:T(8,128)} %param.9) | copy-start | bytes 589828
  65.2 0.6 copy-start.5
  67.4 48.1 %collective-permute-start.4 = (f32[1,2,16,384]{3,2,1,0:T(8,128)S(1)}, f32[1,2,16,384]{3,2,1,0:T(8,128)S(1)}, u32[]{:S(2)}, u32[]{:S(2)}) collective-permute-start(f32[1,2,16,384]{3,2,1,0:T(8,128)S(1)} %get-tuple-element.34), channel_id=1, source_target_pairs={{0,8},{8,16},{16,24},{24,0},{1,9},{9,17},{17,25},{25,1},{2,10},{10... | collective-permute-start | bytes 147464 | tf_op jit(solution)/shard_map/ppermute | solution.py:19
  67.4 48.0 %collective-permute-start.5 = (f32[1,2,16,384]{3,2,1,0:T(8,128)S(1)}, f32[1,2,16,384]{3,2,1,0:T(8,128)S(1)}, u32[]{:S(2)}, u32[]{:S(2)}) collective-permute-start(f32[1,2,16,384]{3,2,1,0:T(8,128)S(1)} %get-tuple-element.35), channel_id=1, source_target_pairs={{8,0},{16,8},{24,16},{0,24},{9,1},{17,9},{25,17},{1,25},{10,2},{18... | collective-permute-start | bytes 147464 | tf_op jit(solution)/shard_map/ppermute | solution.py:22
  115.5 4.0 %collective-permute-start.6 = (f32[1,12,2,384]{3,2,1,0:T(2,128)S(1)}, f32[1,12,2,384]{3,2,1,0:T(2,128)S(1)}, u32[]{:S(2)}, u32[]{:S(2)}) collective-permute-start(f32[1,12,2,384]{3,2,1,0:T(2,128)S(1)} %get-tuple-element.12), channel_id=1, source_target_pairs={{0,4},{4,0},{1,5},{5,1},{2,6},{6,2},{3,7},{7,3},{8,12},{12,8},{9,1... | collective-permute-start | bytes 110600 | tf_op jit(solution)/shard_map/ppermute | solution.py:19
  116.1 4.0 %collective-permute-start.7 = (f32[1,12,2,384]{3,2,1,0:T(2,128)S(1)}, f32[1,12,2,384]{3,2,1,0:T(2,128)S(1)}, u32[]{:S(2)}, u32[]{:S(2)}) collective-permute-start(f32[1,12,2,384]{3,2,1,0:T(2,128)S(1)} %get-tuple-element.13), channel_id=1, source_target_pairs={{4,0},{0,4},{5,1},{1,5},{6,2},{2,6},{7,3},{3,7},{12,8},{8,12},{13,... | collective-permute-start | bytes 110600 | tf_op jit(solution)/shard_map/ppermute | solution.py:22
  120.9 47.8 %collective-permute-start.8 = (f32[1,2,16,384]{3,2,1,0:T(8,128)S(1)}, f32[1,2,16,384]{3,2,1,0:T(8,128)S(1)}, u32[]{:S(2)}, u32[]{:S(2)}) collective-permute-start(f32[1,2,16,384]{3,2,1,0:T(8,128)S(1)} %get-tuple-element.16), channel_id=1, source_target_pairs={{0,8},{8,16},{16,24},{24,0},{1,9},{9,17},{17,25},{25,1},{2,10},{10... | collective-permute-start | bytes 147464 | tf_op jit(solution)/shard_map/ppermute | solution.py:19
  120.9 47.8 %collective-permute-start.9 = (f32[1,2,16,384]{3,2,1,0:T(8,128)S(1)}, f32[1,2,16,384]{3,2,1,0:T(8,128)S(1)}, u32[]{:S(2)}, u32[]{:S(2)}) collective-permute-start(f32[1,2,16,384]{3,2,1,0:T(8,128)S(1)} %get-tuple-element.17), channel_id=1, source_target_pairs={{8,0},{16,8},{24,16},{0,24},{9,1},{17,9},{25,17},{1,25},{10,2},{18... | collective-permute-start | bytes 147464 | tf_op jit(solution)/shard_map/ppermute | solution.py:22
  168.7 4.0 %collective-permute-start.10 = (f32[1,12,2,384]{3,2,1,0:T(2,128)S(1)}, f32[1,12,2,384]{3,2,1,0:T(2,128)S(1)}, u32[]{:S(2)}, u32[]{:S(2)}) collective-permute-start(f32[1,12,2,384]{3,2,1,0:T(2,128)S(1)} %get-tuple-element.10), channel_id=1, source_target_pairs={{0,4},{4,0},{1,5},{5,1},{2,6},{6,2},{3,7},{7,3},{8,12},{12,8},{9,1... | collective-permute-start | bytes 110600 | tf_op jit(solution)/shard_map/ppermute | solution.py:19
  169.6 4.0 %collective-permute-start.11 = (f32[1,12,2,384]{3,2,1,0:T(2,128)S(1)}, f32[1,12,2,384]{3,2,1,0:T(2,128)S(1)}, u32[]{:S(2)}, u32[]{:S(2)}) collective-permute-start(f32[1,12,2,384]{3,2,1,0:T(2,128)S(1)} %get-tuple-element.11), channel_id=1, source_target_pairs={{4,0},{0,4},{5,1},{1,5},{6,2},{2,6},{7,3},{3,7},{12,8},{8,12},{13,... | collective-permute-start | bytes 110600 | tf_op jit(solution)/shard_map/ppermute | solution.py:22
Sparse Core Ops, SparseCore 0:
  176.7 35.6 all-reduce.1
where the time goes:
time: 221 us
  blocking collectives  72.5 us (33%)
  waiting for transfers between devices  41.5 us (19%)
  local copies, waits for them, and re-layouts  39.7 us (18%)
  other arithmetic  31.9 us (14%)
  between operations  14.5 us (7%)
  starting transfers between devices  12.3 us (6%)
  matrix products  8.32 us (4%)
    psum x3, blocking collectives, weights_of(): coef_sums = lax.psum(partial_value, ('gx', 'gy'))  72.5 us
    psum x1, waiting for transfers between devices, local(): density = lax.psum(jnp.sum(filtered * filtered, axis=0), 'orb')  35.8 us
    scatter-add x3, other arithmetic, weights_of(): jax.ops.segment_sum(single, ids_flat, num_segments=count_all)  25.8 us
    gather x3, local copies, waits for them, and re-layouts, weights_of(): return jnp.take(coef_sums * proj_energy[None, :], ids_flat, axis=1)  25.2 us
    ppermute x6, starting transfers between devices, extended(): lax.ppermute(lax.slice_in_dim(block, 0, width, axis=dim), axis, backward)  10 us
  transfers between devices with their start and end apart: 13, of which 7 were waited for; matrix products, arithmetic and copies ran while one was open for 31% of the time, Pallas kernels for 0%

commit v1 on v0

--- a/solution.py
+++ b/solution.py
@@ -67,7 +67,7 @@
         partial_value = jax.vmap(
             lambda single: jax.ops.segment_sum(single, ids_flat, num_segments=count_all)
         )(blocks.reshape(count_orb, -1))
-        coef_sums = lax.psum(partial_value, ("gx", "gy"))
+        coef_sums = jnp.sum(lax.all_gather(partial_value, ("gx", "gy")), axis=0)
         return jnp.take(coef_sums * proj_energy[None, :], ids_flat, axis=1)
 
     def hamilton(grid_vals):

time: 221 us -> 199 us (0.900)
  blocking collectives: 72.5 us -> 49.8 us
    psum x3 -> x0, blocking collectives: 72.5 us -> none  [weights_of(): coef_sums = lax.psum(partial_value, ('gx', 'gy'))]
    all_gather x0 -> x3, blocking collectives: none -> 49.8 us  [weights_of(): coef_sums = jnp.sum(lax.all_gather(partial_value, ('gx', 'gy')), axis=0)]
  transfers between devices with their start and end apart: 13 -> 13, of which waited for: 7 -> 7; matrix products, arithmetic and copies ran while one was open for 31% -> 35% of each run, Pallas kernels for 0% -> 0%
where the time goes in v1:
time: 199 us; the launch traced here: 198 us
  blocking collectives  49.8 us (25%)
  waiting for transfers between devices  41.5 us (21%)
  local copies, waits for them, and re-layouts  39.8 us (20%)
  other arithmetic  32 us (16%)
  between operations  14.6 us (7%)
  starting transfers between devices  12.3 us (6%)
  matrix products  8.32 us (4%)
    all_gather x3, blocking collectives, weights_of(): coef_sums = jnp.sum(lax.all_gather(partial_value, ('gx', 'gy')), axis=0)  49.8 us
    psum x1, waiting for transfers between devices, local(): density = lax.psum(jnp.sum(filtered * filtered, axis=0), 'orb')  35.4 us
    scatter-add x3, other arithmetic, weights_of(): jax.ops.segment_sum(single, ids_flat, num_segments=count_all)  25.8 us
    gather x3, local copies, waits for them, and re-layouts, weights_of(): return jnp.take(coef_sums * proj_energy[None, :], ids_flat, axis=1)  25.2 us
    ppermute x6, starting transfers between devices, extended(): lax.ppermute(lax.slice_in_dim(block, 0, width, axis=dim), axis, backward)  10.4 us
    ppermute x6, waiting for transfers between devices, extended(): lax.ppermute(lax.slice_in_dim(block, block.shape[dim] - width, None, axis...  4.57 us
    dot_general x3, matrix products, hamilton(): jnp.einsum('kxyzb,okxyz->oxyzb', shaped, weights, precision=PRECISE)  4.19 us
    dot_general x3, matrix products, hamilton(): jnp.einsum('kxyzb,oxyzb->okxyz', shaped, grid_vals.reshape(count_orb, ext...  4.12 us
  transfers between devices with their start and end apart: 13, of which 7 were waited for; matrix products, arithmetic and copies ran while one was open for 35% of the time, Pallas kernels for 0%

profile of v1, /device:TPU:0, one launch (start us, length us, event | category | flops | bytes accessed | tf_op | source)
XLA Modules:
  0.0 198.3 jit_solution(8921005641796184764)
XLA Ops:
  6.5 0.9 fusion.72
  7.4 0.5 collective-permute-start
  7.9 2.0 %collective-permute-start.1 = (f32[1,2,16,384]{3,2,1,0:T(8,128)S(1)}, f32[1,2,16,384]{3,2,1,0:T(8,128)S(1)}, u32[]{:S(2)}, u32[]{:S(2)}) collective-permute-start(f32[1,2,16,384]{3,2,1,0:T(8,128)S(1)} %get-tuple-element.39), channel_id=1, source_target_pairs={{8,0},{16,8},{24,16},{0,24},{9,1},{17,9},{25,17},{1,25},{10,2},{18... | collective-permute-start | bytes 147464 | tf_op jit(solution)/shard_map/ppermute | solution.py:22
  9.9 0.2 reshape.516
  10.1 0.1 fusion.74
  10.2 0.1 fusion.76
  10.4 0.8 copy-done.2
  11.3 0.5 copy.11
  11.9 1.4 fusion.78
  13.2 1.0 copy.12
  14.3 0.2 reshape.452
  14.5 0.6 copy-done.4
  15.1 0.3 copy.9
  15.3 0.2 reshape.450
  15.6 8.6 %scatter_custom_fusion = f32[4096]{0:T(1024)S(1)} fusion(s32[1536]{0:T(1024)S(1)} %reshape.450, f32[1536]{0:T(1024)S(1)} %reshape.452, f32[]{:T(128)} %constant.38.clone.1), kind=kCustom, calls=%fused_computation.125 | custom fusion | flops 1536 | bytes 16388 | tf_op jit(solution)/shard_map/vmap()/scatter-add | solution.py:68
  24.2 17.2 %all-gather = f32[32768]{0:T(1024)S(1)} all-gather(f32[4096]{0:T(1024)S(1)} %scatter_custom_fusion), channel_id=2, replica_groups=mesh['gx'=4,'gy'=2,'orb'=4] {'gx','gy'}, dimensions={0}, use_global_device_ids=true | all-gather | bytes 147456 | tf_op jit(solution)/shard_map/all_gather | solution.py:70
  41.5 0.7 copy-done.3
  42.2 8.4 %gather_fusion = f32[1536]{0:T(1024)S(1)} fusion(f32[4096]{0:T(1024)S(1)} %mul.159, s32[2048]{0:T(1024)S(1)} %pad_clamp_fusion), kind=kCustom, calls=%fused_computation.clone | custom fusion | bytes 18432 | tf_op jit(solution)/shard_map/jit(_take)/gather | solution.py:71
  50.6 0.2 reshape.505
  50.8 0.9 copy.13
  51.7 1.4 fusion.79
  53.3 0.5 collective-permute-start.2
  53.8 1.6 collective-permute-start.3
  55.4 0.6 fusion.77
  56.9 0.6 collective-permute-done.2
  57.4 0.7 collective-permute-done.3
  58.1 0.6 copy-done.5
  58.7 1.1 broadcast_multiply_fusion.1
  59.9 0.2 reshape.520
  60.2 0.1 fusion.69
  60.4 1.7 collective-permute-start.5
  62.1 1.4 fusion.80
  63.5 1.0 copy.16
  64.5 0.2 reshape.462
  64.7 8.6 %scatter_custom_fusion.1 = f32[4096]{0:T(1024)S(1)} fusion(s32[1536]{0:T(1024)S(1)} %reshape.450, f32[1536]{0:T(1024)S(1)} %reshape.462, f32[]{:T(128)} %constant.38.clone.1), kind=kCustom, calls=%fused_computation.123 | custom fusion | flops 1536 | bytes 16388 | tf_op jit(solution)/shard_map/vmap()/scatter-add | solution.py:68
  73.3 16.2 %all-gather.1 = f32[32768]{0:T(1024)S(1)} all-gather(f32[4096]{0:T(1024)S(1)} %scatter_custom_fusion.1), channel_id=3, replica_groups=mesh['gx'=4,'gy'=2,'orb'=4] {'gx','gy'}, dimensions={0}, use_global_device_ids=true | all-gather | bytes 147456 | tf_op jit(solution)/shard_map/all_gather | solution.py:70
  89.6 8.4 %gather_fusion.1 = f32[1536]{0:T(1024)S(1)} fusion(f32[4096]{0:T(1024)S(1)} %mul.174, s32[2048]{0:T(1024)S(1)} %pad_clamp_fusion), kind=kCustom, calls=%fused_computation.1.clone | custom fusion | bytes 18432 | tf_op jit(solution)/shard_map/jit(_take)/gather | solution.py:71
  98.0 0.2 reshape.509
  98.2 0.9 copy.17
  99.1 1.4 fusion.81
  100.7 0.4 collective-permute-start.6
  101.1 1.7 collective-permute-start.7
  103.0 2.1 %collective-permute-done.6 = f32[1,12,2,384]{3,2,1,0:T(2,128)S(1)} collective-permute-done((f32[1,12,2,384]{3,2,1,0:T(2,128)S(1)}, f32[1,12,2,384]{3,2,1,0:T(2,128)S(1)}, u32[]{:S(2)}, u32[]{:S(2)}) %collective-permute-start.6) | collective-permute-done | bytes 36896 | tf_op jit(solution)/shard_map/ppermute | solution.py:19
  105.1 0.4 collective-permute-done.7
  105.5 0.3 fusion.30
  105.8 0.2 reshape.524
  106.1 0.1 fusion.66
  106.3 1.7 collective-permute-start.9
  108.0 1.4 fusion.82
  109.4 1.0 copy.20
  110.4 0.2 reshape.472
  110.7 8.6 %scatter_custom_fusion.2 = f32[4096]{0:T(1024)S(1)} fusion(s32[1536]{0:T(1024)S(1)} %reshape.450, f32[1536]{0:T(1024)S(1)} %reshape.472, f32[]{:T(128)} %constant.38.clone.1), kind=kCustom, calls=%fused_computation.121 | custom fusion | flops 1536 | bytes 16388 | tf_op jit(solution)/shard_map/vmap()/scatter-add | solution.py:68
  119.3 16.4 %all-gather.2 = f32[32768]{0:T(1024)S(1)} all-gather(f32[4096]{0:T(1024)S(1)} %scatter_custom_fusion.2), channel_id=4, replica_groups=mesh['gx'=4,'gy'=2,'orb'=4] {'gx','gy'}, dimensions={0}, use_global_device_ids=true | all-gather | bytes 147456 | tf_op jit(solution)/shard_map/all_gather | solution.py:70
  135.7 8.4 %gather_fusion.2 = f32[1536]{0:T(1024)S(1)} fusion(f32[4096]{0:T(1024)S(1)} %mul.188, s32[2048]{0:T(1024)S(1)} %pad_clamp_fusion), kind=kCustom, calls=%fused_computation.2.clone | custom fusion | bytes 18432 | tf_op jit(solution)/shard_map/jit(_take)/gather | solution.py:71
  144.1 0.2 reshape.513
  144.4 0.9 copy.21
  145.2 1.4 fusion.83
  146.8 0.5 collective-permute-start.10
  147.3 1.6 collective-permute-start.11
  149.1 1.9 collective-permute-done.10
  151.1 0.4 collective-permute-done.11
  151.5 3.0 %multiply_bitcast_fusion = f32[8,16,384]{2,1,0:T(8,128)} fusion(f32[1,8,16,384]{3,2,1,0:T(8,128)S(1)} %fusion.30, f32[1,8,16,384]{3,2,1,0:T(8,128)S(1)} %get-tuple-element.7, f32[1,8,16,384]{3,2,1,0:T(8,128)S(1)} %copy-done, f32[1,8,16,384]{3,2,1,0:T(8,128)S(1)} %transpose.23, f32[8,16,384]{2,1,0:T(8,128)S(1)} %copy-done.1, ...), kind=kLoop, calls=%fused_computation.103 | loop fusion | flops 2605056 | bytes 2138128 | tf_op jit(solution)/shard_map/reduce_sum | solution.py:98
  154.5 35.4 %all-reduce.2.cloned.1.call-done = f32[8,16,384]{2,1,0:T(8,128)} async-done(((f32[8,16,384]{2,1,0:T(8,128)}), f32[8,16,384]{2,1,0:T(8,128)}) %all-reduce.2.cloned.1.call-update) | async-done | bytes 196624 | tf_op jit(solution)/shard_map/psum | solution.py:98
  189.8 1.6 broadcast_multiply_fusion
  (57 shorter events, 1.9 us)
Async XLA Ops:
  6.5 3.4 %copy-start = (f32[1,8,16,384]{3,2,1,0:T(8,128)S(1)}, f32[1,8,16,384]{3,2,1,0:T(8,128)}, u32[]{:S(2)}) copy-start(f32[1,8,16,384]{3,2,1,0:T(8,128)} %param.8) | copy-start | bytes 589828
  6.5 183.3 %all-reduce.2.cloned.1.call-start = ((), (), s32[]{:S(2)}) async-start(), calls=%async_computation | async-start | bytes 393216 | tf_op jit(solution)/shard_map/psum | solution.py:98
  7.4 45.7 %collective-permute-start = (f32[1,2,16,384]{3,2,1,0:T(8,128)S(1)}, f32[1,2,16,384]{3,2,1,0:T(8,128)S(1)}, u32[]{:S(2)}, u32[]{:S(2)}) collective-permute-start(f32[1,2,16,384]{3,2,1,0:T(8,128)S(1)} %get-tuple-element.40), channel_id=1, source_target_pairs={{0,8},{8,16},{16,24},{24,0},{1,9},{9,17},{17,25},{25,1},{2,10},{10... | collective-permute-start | bytes 147464 | tf_op jit(solution)/shard_map/ppermute | solution.py:19
  7.9 45.3 %collective-permute-start.1 = (f32[1,2,16,384]{3,2,1,0:T(8,128)S(1)}, f32[1,2,16,384]{3,2,1,0:T(8,128)S(1)}, u32[]{:S(2)}, u32[]{:S(2)}) collective-permute-start(f32[1,2,16,384]{3,2,1,0:T(8,128)S(1)} %get-tuple-element.39), channel_id=1, source_target_pairs={{8,0},{16,8},{24,16},{0,24},{9,1},{17,9},{25,17},{1,25},{10,2},{18... | collective-permute-start | bytes 147464 | tf_op jit(solution)/shard_map/ppermute | solution.py:22
  10.2 1.0 copy-start.2
  14.3 0.8 copy-start.4
  41.4 0.7 copy-start.3
  53.3 2.1 %copy-start.6 = (f32[4]{0:T(128)S(1)}, f32[4]{0:T(128)}, u32[]{:S(2)}) copy-start(f32[4]{0:T(128)} %param.13) | copy-start | bytes 52
  53.3 4.1 %collective-permute-start.2 = (f32[1,12,2,384]{3,2,1,0:T(2,128)S(1)}, f32[1,12,2,384]{3,2,1,0:T(2,128)S(1)}, u32[]{:S(2)}, u32[]{:S(2)}) collective-permute-start(f32[1,12,2,384]{3,2,1,0:T(2,128)S(1)} %get-tuple-element.14), channel_id=1, source_target_pairs={{0,4},{4,0},{1,5},{5,1},{2,6},{6,2},{3,7},{7,3},{8,12},{12,8},{9,1... | collective-permute-start | bytes 110600 | tf_op jit(solution)/shard_map/ppermute | solution.py:19
  53.8 4.4 %collective-permute-start.3 = (f32[1,12,2,384]{3,2,1,0:T(2,128)S(1)}, f32[1,12,2,384]{3,2,1,0:T(2,128)S(1)}, u32[]{:S(2)}, u32[]{:S(2)}) collective-permute-start(f32[1,12,2,384]{3,2,1,0:T(2,128)S(1)} %get-tuple-element.15), channel_id=1, source_target_pairs={{4,0},{0,4},{5,1},{1,5},{6,2},{2,6},{7,3},{3,7},{12,8},{8,12},{13,... | collective-permute-start | bytes 110600 | tf_op jit(solution)/shard_map/ppermute | solution.py:22
  56.1 2.6 %copy-start.1 = (f32[8,16,384]{2,1,0:T(8,128)S(1)}, f32[8,16,384]{2,1,0:T(8,128)}, u32[]{:S(2)}) copy-start(f32[8,16,384]{2,1,0:T(8,128)} %param.9) | copy-start | bytes 589828
  58.1 0.6 copy-start.5
  60.3 40.3 %collective-permute-start.4 = (f32[1,2,16,384]{3,2,1,0:T(8,128)S(1)}, f32[1,2,16,384]{3,2,1,0:T(8,128)S(1)}, u32[]{:S(2)}, u32[]{:S(2)}) collective-permute-start(f32[1,2,16,384]{3,2,1,0:T(8,128)S(1)} %get-tuple-element.34), channel_id=1, source_target_pairs={{0,8},{8,16},{16,24},{24,0},{1,9},{9,17},{17,25},{25,1},{2,10},{10... | collective-permute-start | bytes 147464 | tf_op jit(solution)/shard_map/ppermute | solution.py:19
  60.4 40.3 %collective-permute-start.5 = (f32[1,2,16,384]{3,2,1,0:T(8,128)S(1)}, f32[1,2,16,384]{3,2,1,0:T(8,128)S(1)}, u32[]{:S(2)}, u32[]{:S(2)}) collective-permute-start(f32[1,2,16,384]{3,2,1,0:T(8,128)S(1)} %get-tuple-element.35), channel_id=1, source_target_pairs={{8,0},{16,8},{24,16},{0,24},{9,1},{17,9},{25,17},{1,25},{10,2},{18... | collective-permute-start | bytes 147464 | tf_op jit(solution)/shard_map/ppermute | solution.py:22
  100.7 4.4 %collective-permute-start.6 = (f32[1,12,2,384]{3,2,1,0:T(2,128)S(1)}, f32[1,12,2,384]{3,2,1,0:T(2,128)S(1)}, u32[]{:S(2)}, u32[]{:S(2)}) collective-permute-start(f32[1,12,2,384]{3,2,1,0:T(2,128)S(1)} %get-tuple-element.12), channel_id=1, source_target_pairs={{0,4},{4,0},{1,5},{5,1},{2,6},{6,2},{3,7},{7,3},{8,12},{12,8},{9,1... | collective-permute-start | bytes 110600 | tf_op jit(solution)/shard_map/ppermute | solution.py:19
  101.1 4.4 %collective-permute-start.7 = (f32[1,12,2,384]{3,2,1,0:T(2,128)S(1)}, f32[1,12,2,384]{3,2,1,0:T(2,128)S(1)}, u32[]{:S(2)}, u32[]{:S(2)}) collective-permute-start(f32[1,12,2,384]{3,2,1,0:T(2,128)S(1)} %get-tuple-element.13), channel_id=1, source_target_pairs={{4,0},{0,4},{5,1},{1,5},{6,2},{2,6},{7,3},{3,7},{12,8},{8,12},{13,... | collective-permute-start | bytes 110600 | tf_op jit(solution)/shard_map/ppermute | solution.py:22
  106.2 40.5 %collective-permute-start.8 = (f32[1,2,16,384]{3,2,1,0:T(8,128)S(1)}, f32[1,2,16,384]{3,2,1,0:T(8,128)S(1)}, u32[]{:S(2)}, u32[]{:S(2)}) collective-permute-start(f32[1,2,16,384]{3,2,1,0:T(8,128)S(1)} %get-tuple-element.16), channel_id=1, source_target_pairs={{0,8},{8,16},{16,24},{24,0},{1,9},{9,17},{17,25},{25,1},{2,10},{10... | collective-permute-start | bytes 147464 | tf_op jit(solution)/shard_map/ppermute | solution.py:19
  106.3 40.4 %collective-permute-start.9 = (f32[1,2,16,384]{3,2,1,0:T(8,128)S(1)}, f32[1,2,16,384]{3,2,1,0:T(8,128)S(1)}, u32[]{:S(2)}, u32[]{:S(2)}) collective-permute-start(f32[1,2,16,384]{3,2,1,0:T(8,128)S(1)} %get-tuple-element.17), channel_id=1, source_target_pairs={{8,0},{16,8},{24,16},{0,24},{9,1},{17,9},{25,17},{1,25},{10,2},{18... | collective-permute-start | bytes 147464 | tf_op jit(solution)/shard_map/ppermute | solution.py:22
  146.8 4.3 %collective-permute-start.10 = (f32[1,12,2,384]{3,2,1,0:T(2,128)S(1)}, f32[1,12,2,384]{3,2,1,0:T(2,128)S(1)}, u32[]{:S(2)}, u32[]{:S(2)}) collective-permute-start(f32[1,12,2,384]{3,2,1,0:T(2,128)S(1)} %get-tuple-element.10), channel_id=1, source_target_pairs={{0,4},{4,0},{1,5},{5,1},{2,6},{6,2},{3,7},{7,3},{8,12},{12,8},{9,1... | collective-permute-start | bytes 110600 | tf_op jit(solution)/shard_map/ppermute | solution.py:19
  147.3 4.2 %collective-permute-start.11 = (f32[1,12,2,384]{3,2,1,0:T(2,128)S(1)}, f32[1,12,2,384]{3,2,1,0:T(2,128)S(1)}, u32[]{:S(2)}, u32[]{:S(2)}) collective-permute-start(f32[1,12,2,384]{3,2,1,0:T(2,128)S(1)} %get-tuple-element.11), channel_id=1, source_target_pairs={{4,0},{0,4},{5,1},{1,5},{6,2},{2,6},{7,3},{3,7},{12,8},{8,12},{13,... | collective-permute-start | bytes 110600 | tf_op jit(solution)/shard_map/ppermute | solution.py:22
Sparse Core Ops, SparseCore 0:
  154.6 35.2 all-reduce.1
